TPU v7x, 256 devices: a whole 4x4x8 slice. The times are simulated.
256 devices in a mesh: dp: 16 (over x, y), expert: 16 (over z, core).
Axes of the slice: x: 4, y: 4, z: 8, core: 2. Of those that a mesh axis runs over, the one named last changes fastest.
Arguments:
- hidden: bfloat16 [16, 16, 384, 1024], P('dp', 'expert'), may hold values from -6 to 6
- down_weight: bfloat16 [16, 1024, 3584], P('expert'), may hold values from -0.1875 to 0.1875
- cotangent: bfloat16 [8192, 3584], P('dp', 'expert'), may hold values from -6 to 6
- expert_ids: int32 [8192, 8], P('dp'), may hold values from 0 to 15, as said below
- gate_weights: bfloat16 [8192, 8], P('dp'), may hold values from 0.049804688 to 0.5
- row_token: int32 [16, 16, 384], P('dp', 'expert'), may hold values from -1 to 511, as said below
- tile_count: int32 [16, 16], P('dp', 'expert'), may hold values from 1 to 3, as said below
Outputs:
- mixed_out: bfloat16 [8192, 3584], P('dp', 'expert')
- hidden_grad: bfloat16 [16, 16, 384, 1024], P('dp', 'expert')
- weight_grad: float32 [16, 1024, 3584], P('expert', 'dp')
Inputs may be any that keep to these rules, and one draw needn't show every extreme that they name: `expert_ids`: each token names 8 different experts; every expert is named by some token of every group. row_token[i, e, r] is the index within group i (0 to 511) of a token that names expert e, or -1 for an empty slot; each token of a group stands exactly once in the rows of each expert it names and nowhere else; an expert's filled rows come first. tile_count[i, e] is the number of 128-row tiles that hold expert e's filled rows in group i, except for one expert of every group whose count is one tile less; the busiest expert of every group has 384 filled rows, all of them counted.
All inputs are finite; a program needn't handle non-finite values.
Results may differ from a plain program's by a relative error of at most 0.013.
Values may be sent and summed in bfloat16 or wider, within the bound.
A program may use at most 128 MiB of HBM per device.

v0:
```python
import jax
import jax.numpy as jnp
from jax import lax
from jax.sharding import PartitionSpec as P

EXPERTS = 16
TILE = 128


def swapped(shard, axis, bit):
    return lax.ppermute(shard, axis, [(i, i ^ 1 << bit) for i in range(lax.axis_size(axis))])


def tile_products(rows_in, weight_mat, count, contract_dim):
    rows_cap = rows_in.shape[0]
    width_out = weight_mat.shape[1 - contract_dim]

    def one_tile(tile_index, outputs):
        block = lax.dynamic_slice_in_dim(rows_in, tile_index * TILE, TILE, 0)
        product = lax.dot_general(
            block,
            weight_mat,
            (((1,), (contract_dim,)), ((), ())),
            preferred_element_type=jnp.float32,
        )
        return lax.dynamic_update_slice_in_dim(
            outputs, product.astype(jnp.bfloat16), tile_index * TILE, 0
        )

    return lax.fori_loop(0, count, one_tile, jnp.zeros((rows_cap, width_out), jnp.bfloat16))


def body(hidden, down_weight, cotangent, expert_ids, gate_weights, row_token, tile_count):
    local_count = down_weight.shape[0]
    group_size = cotangent.shape[0]
    expert_index = jnp.arange(EXPERTS, dtype=jnp.int32)
    named_cols = expert_ids[:, :, None] == expert_index[None, None, :]
    gate_cols = jnp.sum(
        jnp.where(named_cols, gate_weights[:, :, None].astype(jnp.float32), 0.0), axis=1
    ).astype(jnp.bfloat16)
    group_cot = lax.all_gather(cotangent, "expert", axis=1, tiled=True)
    width = group_cot.shape[1]
    first_expert = lax.axis_index("expert") * local_count
    slot_index = jnp.arange(hidden.shape[2], dtype=jnp.int32)
    share_rows = down_weight.shape[1] // lax.axis_size("dp")
    partial_value = jnp.zeros((group_size, width), jnp.float32)
    token_rows = row_token[0, 0]
    count = tile_count[0, 0]
    live_rows = (token_rows >= 0) & (slot_index < count * TILE)
    safe_rows = jnp.where(live_rows, token_rows, 0)
    column = lax.dynamic_index_in_dim(gate_cols, first_expert + 0, 1, keepdims=False)
    row_gate = jnp.where(live_rows, column[safe_rows].astype(jnp.float32), 0.0)
    target = jnp.where(live_rows, token_rows, group_size)
    hidden_rows = hidden[0, 0]
    weight_mat = down_weight[0]
    out_rows = tile_products(hidden_rows, weight_mat, count, 0)
    partial_value = partial_value.at[target].add(
        row_gate[:, None] * out_rows.astype(jnp.float32), mode="drop"
    )
    routed = (row_gate[:, None] * group_cot[safe_rows].astype(jnp.float32)).astype(jnp.bfloat16)
    grad_list = [tile_products(routed, weight_mat, count, 1)]

    def weight_rows(start, rows_count, hidden_rows=hidden_rows, routed_rows=routed):
        return lax.dot_general(
            hidden_rows, routed_rows, (((0,), (0,)), ((), ())), preferred_element_type=jnp.float32
        )

    weight_list = [
        lax.psum_scatter(
            weight_rows(jnp.int32(0), share_rows * lax.axis_size("dp")).astype(jnp.bfloat16),
            "dp",
            scatter_dimension=0,
            tiled=True,
        ).astype(jnp.float32)
    ]
    merged = partial_value
    top_bit = lax.axis_size("expert").bit_length() - 1
    axis_index = lax.axis_index("expert")
    for bit_index in reversed(range(top_bit)):
        half_cols = merged.shape[1] // 2
        lower_half = merged[:, :half_cols]
        upper_half = merged[:, half_cols:]
        high_side = axis_index // 2**bit_index % 2 == 1
        sending = jnp.where(high_side, lower_half, upper_half)
        keeping = jnp.where(high_side, upper_half, lower_half)
        merged = keeping + swapped(sending.astype(jnp.bfloat16), "expert", bit_index).astype(
            sending.dtype
        )
    mixed_out = merged.astype(jnp.bfloat16)
    hidden_grad = jnp.stack(grad_list, axis=0)[None]
    weight_grad = jnp.stack(weight_list, axis=0)
    return (mixed_out, hidden_grad, weight_grad)


def solution(mesh):
    placed = (
        P("dp", "expert", None, None),
        P("expert", None, None),
        P("dp", "expert"),
        P("dp", None),
        P("dp", None),
        P("dp", "expert", None),
        P("dp", "expert"),
    )
    return jax.shard_map(
        body,
        mesh=mesh,
        in_specs=placed,
        out_specs=(P("dp", "expert"), P("dp", "expert", None, None), P("expert", "dp", None)),
        check_vma=False,
    )
```

profile of v0, /device:TPU:8, one launch (start us, length us, event | category | flops | bytes accessed | tf_op | source)
XLA Modules:
  0.0 311.5 jit_solution(3200420147319569231)
XLA Ops:
  7.2 0.0 all-gather.2.cloned.1.call-start
  7.2 0.7 all-gather.2.cloned.1.call-update
  7.9 0.0 reduce-scatter.4.cloned.1.call-start
  8.0 0.7 convert_element_type.63
  9.3 0.8 select_reduce_fusion
  10.1 0.7 fusion.15
  10.8 2.8 gather_fusion
  13.6 0.7 compare_reduce_fusion
  14.3 39.7 %all-gather.2.cloned.1.call-done = bf16[512,3584]{0,1:T(8,128)(2,1)} async-done(((bf16[512,224]{0,1:T(8,128)(2,1)}), bf16[512,3584]{0,1:T(8,128)(2,1)}) %all-gather.2.cloned.1.call-update) | async-done | bytes 3670032 | tf_op jit(solution)/shard_map/all_gather | solution.py:41
  54.0 6.0 %copy.24 = bf16[512,3584]{1,0:T(8,128)(2,1)} copy(bf16[512,3584]{0,1:T(8,128)(2,1)} %all-gather.2.cloned.1.call-done) | data formatting | bytes 7340032 | tf_op jit(solution)/shard_map/all_gather | solution.py:41
  60.0 10.1 %gather_fusion.1 = bf16[384,3584]{1,0:T(8,128)(2,1)} fusion(bf16[512,3584]{1,0:T(8,128)(2,1)} %copy.24, s32[1024]{0:T(1024)S(1)} %pad_clamp_fusion), kind=kCustom, calls=%fused_computation.1 | custom fusion | bytes 5506560 | tf_op jit(solution)/shard_map/gather | solution.py:60
  70.1 2.6 multiply_convert_fusion
  72.8 6.2 %fusion.6 = bf16[1024,3584]{0,1:T(8,128)(2,1)} fusion(bf16[384,3584]{1,0:T(8,128)(2,1)S(1)} %multiply_convert_fusion, bf16[1,1,384,1024]{3,2,1,0:T(8,128)(2,1)S(1)} %copy-done.3), kind=kOutput, calls=%fused_computation.12 | convolution fusion | flops 2822242304 | bytes 10878976 | tf_op jit(solution)/shard_map/dot_general | solution.py:64
  79.0 10.0 %copy.27 = bf16[1024,3584]{1,0:T(8,128)(2,1)} copy(bf16[1024,3584]{0,1:T(8,128)(2,1)} %fusion.6) | data formatting | bytes 14680064
  89.0 1.7 broadcast_in_dim.43
  90.7 18.7 %while.20 = (s32[]{:T(128)}, bf16[384,3584]{1,0:T(8,128)(2,1)}, s32[]{:T(128)}, bf16[384,1024]{1,0:T(8,128)(2,1)S(1)}, bf16[1024,3584]{1,0:T(8,128)(2,1)}, /*index=5*/s32[]{:T(128)}, s32[]{:T(128)}, s32[]{:T(128)}, s32[]{:T(128)}) while((s32[]{:T(128)}, bf16[384,3584]{1,0:T(8,128)(2,1)}, s32[]{:T(128)}, bf16[384,1024]{1,0:T(8,128)(2,1)S(1)}, ...), condition=%wide.region_2.3_spmd, body=%wide.region_1.2_spmd.sunk | while | flops 939982848 | bytes 8520843 | solution.py:30
  91.4 5.1 %fusion.28 = bf16[384,3584]{1,0:T(8,128)(2,1)} fusion(bf16[384,3584]{1,0:T(8,128)(2,1)} %get-tuple-element.169, s32[]{:T(128)S(6)} %select_n.202, bf16[1024,3584]{1,0:T(8,128)(2,1)} %get-tuple-element.181, bf16[384,1024]{1,0:T(8,128)(2,1)S(1)} %get-tuple-element.180), kind=kOutput, calls=%fused_computation.4.clone.1 | convolution fusion | flops 939982848 | bytes 8520704 | tf_op jit(solution)/shard_map/while/body/dot_general | solution.py:20
  97.2 5.5 %fusion.28 = bf16[384,3584]{1,0:T(8,128)(2,1)} fusion(bf16[384,3584]{1,0:T(8,128)(2,1)} %get-tuple-element.169, s32[]{:T(128)S(6)} %select_n.202, bf16[1024,3584]{1,0:T(8,128)(2,1)} %get-tuple-element.181, bf16[384,1024]{1,0:T(8,128)(2,1)S(1)} %get-tuple-element.180), kind=kOutput, calls=%fused_computation.4.clone.1 | convolution fusion | flops 939982848 | bytes 8520704 | tf_op jit(solution)/shard_map/while/body/dot_general | solution.py:20
  103.3 5.2 %fusion.28 = bf16[384,3584]{1,0:T(8,128)(2,1)} fusion(bf16[384,3584]{1,0:T(8,128)(2,1)} %get-tuple-element.169, s32[]{:T(128)S(6)} %select_n.202, bf16[1024,3584]{1,0:T(8,128)(2,1)} %get-tuple-element.181, bf16[384,1024]{1,0:T(8,128)(2,1)S(1)} %get-tuple-element.180), kind=kOutput, calls=%fused_computation.4.clone.1 | convolution fusion | flops 939982848 | bytes 8520704 | tf_op jit(solution)/shard_map/while/body/dot_general | solution.py:20
  109.4 12.8 %scatter_custom_fusion = f32[512,3584]{1,0:T(8,128)} fusion(s32[384]{0:T(512)S(1)} %get-tuple-element.74, bf16[384,3584]{1,0:T(8,128)(2,1)} %get-tuple-element.59, f32[]{:T(128)} %constant.98.clone.1, f32[384]{0:T(512)S(1)} %convert_select_fusion), kind=kCustom, calls=%fused_computation.14 | custom fusion | flops 4128768 | bytes 10094596 | tf_op jit(solution)/shard_map/scatter-add | solution.py:57
  122.2 4.8 %select_convert_fusion = bf16[512,1792]{1,0:T(8,128)(2,1)} fusion(f32[512,3584]{1,0:T(8,128)} %scatter_custom_fusion, pred[]{:T(512)S(6)} %eq.33), kind=kLoop, calls=%fused_computation.18 | loop fusion | flops 917504 | bytes 5505025 | tf_op jit(solution)/shard_map/convert_element_type | solution.py:86
  126.9 41.3 %collective-permute-done = bf16[512,1792]{1,0:T(8,128)(2,1)} collective-permute-done((bf16[512,1792]{1,0:T(8,128)(2,1)}, bf16[512,1792]{1,0:T(8,128)(2,1)}, u32[]{:S(2)}, u32[]{:S(2)}) %collective-permute-start) | collective-permute-done | bytes 1835040 | tf_op jit(solution)/shard_map/ppermute | solution.py:11
  168.2 4.3 %convert_add_fusion = f32[512,1792]{1,0:T(8,128)S(1)} fusion(bf16[512,1792]{1,0:T(8,128)(2,1)} %collective-permute-done, f32[512,3584]{1,0:T(8,128)} %scatter_custom_fusion, pred[]{:T(512)S(6)} %eq.33), kind=kLoop, calls=%fused_computation.17 | loop fusion | flops 2752512 | bytes 12845057 | tf_op jit(solution)/shard_map/add | solution.py:86
  172.6 1.9 copy-done
  174.5 1.1 select_convert_fusion.1
  175.6 40.9 %collective-permute-start.1 = (bf16[512,896]{1,0:T(8,128)(2,1)}, bf16[512,896]{1,0:T(8,128)(2,1)}, u32[]{:S(2)}, u32[]{:S(2)}) collective-permute-start(bf16[512,896]{1,0:T(8,128)(2,1)} %select_convert_fusion.1), channel_id=1, source_target_pairs={{0,4},{1,5},{2,6},{3,7},{4,0},{5,1},{6,2},{7,3},{8,12},{9,13},{10,... | collective-permute-start | bytes 2752520 | tf_op jit(solution)/shard_map/ppermute | solution.py:11
  216.5 40.6 %collective-permute-done.1 = bf16[512,896]{1,0:T(8,128)(2,1)} collective-permute-done((bf16[512,896]{1,0:T(8,128)(2,1)}, bf16[512,896]{1,0:T(8,128)(2,1)}, u32[]{:S(2)}, u32[]{:S(2)}) %collective-permute-start.1) | collective-permute-done | bytes 917536 | tf_op jit(solution)/shard_map/ppermute | solution.py:11
  257.0 2.6 convert_add_fusion.1
  259.6 1.3 copy-done.1
  260.9 0.2 select_convert_fusion.2
  261.1 1.0 collective-permute-start.2
  262.1 12.8 %collective-permute-done.2 = bf16[512,448]{1,0:T(8,128)(2,1)} collective-permute-done((bf16[512,448]{1,0:T(8,128)(2,1)S(1)}, bf16[512,448]{1,0:T(8,128)(2,1)}, u32[]{:S(2)}, u32[]{:S(2)}) %collective-permute-start.2) | collective-permute-done | bytes 458784 | tf_op jit(solution)/shard_map/ppermute | solution.py:11
  274.9 2.0 convert_add_fusion.2
  276.9 1.0 copy-done.2
  277.9 0.1 select_convert_fusion.3
  278.0 0.1 collective-permute-start.3
  278.1 1.5 collective-permute-done.3
  279.7 1.5 add_convert_fusion
  281.2 0.8 copy.25
  282.0 0.1 broadcast_in_dim.44
  282.1 19.3 %while.21 = (s32[]{:T(128)}, bf16[384,1024]{1,0:T(8,128)(2,1)S(1)}, s32[]{:T(128)}, bf16[384,3584]{1,0:T(8,128)(2,1)S(1)}, bf16[1024,3584]{1,0:T(8,128)(2,1)}, /*index=5*/s32[]{:T(128)}, s32[]{:T(128)}, s32[]{:T(128)}, s32[]{:T(128)}) while((s32[]{:T(128)}, bf16[384,1024]{1,0:T(8,128)(2,1)S(1)}, s32[]{:T(128)}, ...), condition=%wide.region_5.6_spmd, body=%wide.region_4.5_spmd.sunk | while | flops 939655168 | bytes 8520843 | solution.py:30
  282.8 5.5 %fusion.31 = bf16[384,1024]{1,0:T(8,128)(2,1)S(1)} fusion(bf16[384,1024]{1,0:T(8,128)(2,1)S(1)} %get-tuple-element.196, s32[]{:T(128)S(6)} %select_n.203, bf16[1024,3584]{1,0:T(8,128)(2,1)} %get-tuple-element.208, bf16[384,3584]{1,0:T(8,128)(2,1)S(1)} %get-tuple-element.207), kind=kOutput, calls=%fused_computation.8.clone.1 | convolution fusion | flops 939655168 | bytes 8520704 | tf_op jit(solution)/shard_map/while/body/dot_general | solution.py:20
  288.9 5.5 %fusion.31 = bf16[384,1024]{1,0:T(8,128)(2,1)S(1)} fusion(bf16[384,1024]{1,0:T(8,128)(2,1)S(1)} %get-tuple-element.196, s32[]{:T(128)S(6)} %select_n.203, bf16[1024,3584]{1,0:T(8,128)(2,1)} %get-tuple-element.208, bf16[384,3584]{1,0:T(8,128)(2,1)S(1)} %get-tuple-element.207), kind=kOutput, calls=%fused_computation.8.clone.1 | convolution fusion | flops 939655168 | bytes 8520704 | tf_op jit(solution)/shard_map/while/body/dot_general | solution.py:20
  295.2 5.5 %fusion.31 = bf16[384,1024]{1,0:T(8,128)(2,1)S(1)} fusion(bf16[384,1024]{1,0:T(8,128)(2,1)S(1)} %get-tuple-element.196, s32[]{:T(128)S(6)} %select_n.203, bf16[1024,3584]{1,0:T(8,128)(2,1)} %get-tuple-element.208, bf16[384,3584]{1,0:T(8,128)(2,1)S(1)} %get-tuple-element.207), kind=kOutput, calls=%fused_computation.8.clone.1 | convolution fusion | flops 939655168 | bytes 8520704 | tf_op jit(solution)/shard_map/while/body/dot_general | solution.py:20
  301.4 0.0 reduce-scatter.4.cloned.1.call-done
  301.4 1.7 copy.28
  303.1 0.1 bitcast_convert_fusion
  303.2 1.4 copy.26
  (12 shorter events, 0.1 us)
Async XLA Ops:
  7.2 46.9 %all-gather.2.cloned.1.call-start = ((), (), s32[]{:S(2)}) async-start(), calls=%async_computation.1 | async-start | bytes 3899392 | tf_op jit(solution)/shard_map/all_gather | solution.py:41
  7.9 293.5 %reduce-scatter.4.cloned.1.call-start = ((), (), s32[]{:S(2)}) async-start(), calls=%async_computation.2 | async-start | bytes 7798784
  70.1 2.7 copy-start.3
  126.9 41.3 %collective-permute-start = (bf16[512,1792]{1,0:T(8,128)(2,1)}, bf16[512,1792]{1,0:T(8,128)(2,1)}, u32[]{:S(2)}, u32[]{:S(2)}) collective-permute-start(bf16[512,1792]{1,0:T(8,128)(2,1)} %select_convert_fusion), channel_id=1, source_target_pairs={{0,8},{1,9},{2,10},{3,11},{4,12},{5,13},{6,14},{7,15},{8,0},{9,1},... | collective-permute-start | bytes 5505032 | tf_op jit(solution)/shard_map/ppermute | solution.py:11
  172.6 1.9 copy-start
  175.6 81.5 %collective-permute-start.1 = (bf16[512,896]{1,0:T(8,128)(2,1)}, bf16[512,896]{1,0:T(8,128)(2,1)}, u32[]{:S(2)}, u32[]{:S(2)}) collective-permute-start(bf16[512,896]{1,0:T(8,128)(2,1)} %select_convert_fusion.1), channel_id=1, source_target_pairs={{0,4},{1,5},{2,6},{3,7},{4,0},{5,1},{6,2},{7,3},{8,12},{9,13},{10,... | collective-permute-start | bytes 2752520 | tf_op jit(solution)/shard_map/ppermute | solution.py:11
  259.6 1.3 copy-start.1
  261.1 13.7 %collective-permute-start.2 = (bf16[512,448]{1,0:T(8,128)(2,1)S(1)}, bf16[512,448]{1,0:T(8,128)(2,1)}, u32[]{:S(2)}, u32[]{:S(2)}) collective-permute-start(bf16[512,448]{1,0:T(8,128)(2,1)S(1)} %select_convert_fusion.2), channel_id=1, source_target_pairs={{0,2},{1,3},{2,0},{3,1},{4,6},{5,7},{6,4},{7,5},{8,10},{9,11},{10,... | collective-permute-start | bytes 1376264 | tf_op jit(solution)/shard_map/ppermute | solution.py:11
  276.9 1.0 copy-start.2
  278.0 1.6 collective-permute-start.3
  301.3 3.3 %copy-start.4 = (bf16[384,1024]{1,0:T(8,128)(2,1)}, bf16[384,1024]{1,0:T(8,128)(2,1)S(1)}, u32[]{:S(2)}) copy-start(bf16[384,1024]{1,0:T(8,128)(2,1)S(1)} %get-tuple-element.60) | copy-start | bytes 2359300
Sparse Core Ops, SparseCore 0:
  9.8 44.1 all-gather.1
  89.1 87.1 reduce-scatter.3
where the time goes:
time: 316 us; the launch traced here: 312 us
  waiting for transfers between devices  137 us (43%)
  starting transfers between devices  42 us (13%)
  local copies, waits for them, and re-layouts  38.9 us (12%)
  matrix products  38.6 us (12%)
  other arithmetic  35.1 us (11%)
  between operations  14.9 us (5%)
  loops' own time  5.5 us (2%)
    ppermute x4, waiting for transfers between devices, swapped(): lax.ppermute(shard, axis, [(i, i ^ 1 << bit) for i in range(lax.axis_size...  96.2 us
    ppermute x4, starting transfers between devices, swapped(): lax.ppermute(shard, axis, [(i, i ^ 1 << bit) for i in range(lax.axis_size...  42 us
    all_gather x1, waiting for transfers between devices, body(): group_cot = lax.all_gather(cotangent, 'expert', axis=1, tiled=True)  39.7 us
    dot_general x6, matrix products, one_tile(): lax.dot_general(block, weight_mat, (((1,), (contract_dim,)), ((), ())), p...  32.4 us
    unnamed x14, local copies, waits for them, and re-layouts  18.2 us
    scatter-add x1, other arithmetic, body(): partial_value.at[target]  12.8 us
    gather x1, local copies, waits for them, and re-layouts, body(): group_cot[safe_rows].astype(jnp.float32)  10.1 us
    add x3, other arithmetic, body(): keeping + swapped(sending.astype(jnp.bfloat16), 'expert', bit_index).asty...  8.92 us
  transfers between devices with their start and end apart: 6, of which 5 were waited for; matrix products, arithmetic and copies ran while one was open for 23% of the time, Pallas kernels for 0%

commit v1 on v0

v1 whole, which is shorter than its diff:
```python
import jax
import jax.numpy as jnp
from jax import lax
from jax.experimental import pallas as pl
from jax.experimental.pallas import tpu as pltpu
from jax.sharding import PartitionSpec as P

MESH = pl.DeviceIdType.MESH
ROWS, HID, DIM, TOK = 384, 1024, 3584, 512
NZ = 8
BLK, SUB, ZBL, PAIR = 224, 112, 448, 896
WIDTHS = (512, 896, 896, 896, 512)
NT = (((1,), (1,)), ((), ()))
NN = (((1,), (0,)), ((), ()))
TN = (((0,), (0,)), ((), ()))
BF, F32 = jnp.bfloat16, jnp.float32
N_COPIES = 128


def dot(a, b, dims):
    return lax.dot_general(a, b, dims, preferred_element_type=F32)


def eye(n):
    return (
        lax.broadcasted_iota(jnp.int32, (n, n), 0) == lax.broadcasted_iota(jnp.int32, (n, n), 1)
    ).astype(F32).astype(BF)


def kernel(*refs):
    (hid_h, w_h, cot_h, ids_h, gw_h, tok_h, cnt_s, mix_o, hg_o, wg_o) = refs[:10]
    it = iter(refs[10:])
    nxt = lambda: next(it)
    hid, hT, hP, w, cot, ids, gw, tok, GT, cotT, RT = (nxt() for _ in range(11))
    PB = [nxt() for _ in range(5)]
    RF = [nxt() for _ in range(5)]
    RN = [nxt() for _ in range(5)]
    S2 = [nxt() for _ in range(5)]
    RF2 = [nxt() for _ in range(5)]
    RN2 = [nxt() for _ in range(5)]
    FB = [nxt() for _ in range(5)]
    OZ, wgb, M, MR, ZS, ZR, acc, hgb, mixb, mixT = (nxt() for _ in range(10))
    send_sem, recv_sem, loc_sem = (nxt() for _ in range(3))

    dpi, ei = lax.axis_index("dp"), lax.axis_index("expert")
    x, y, z, c = dpi // 4, dpi % 4, ei // 2, ei % 2
    m1 = (1 - c) * x + c * y
    m2 = (1 - c) * y + c * x

    def dpid(p1, p2):
        return (1 - c) * (p1 * 4 + p2) + c * (p2 * 4 + p1)

    def zz(s):
        return (z + s + NZ) % NZ

    n1p = (dpid((m1 + 1) % 4, m2), ei)
    n1m = (dpid((m1 + 3) % 4, m2), ei)
    n2p = (dpid(m1, (m2 + 1) % 4), ei)
    n2m = (dpid(m1, (m2 + 3) % 4), ei)
    zp = (dpi, zz(1) * 2 + c)
    zm = (dpi, zz(-1) * 2 + c)
    pt = (dpi, z * 2 + 1 - c)

    loads = {}

    def load(name, src, dst):
        cp = pltpu.make_async_copy(src, dst, loc_sem.at[len(loads)])
        cp.start()
        loads[name] = cp

    load("cot", cot_h, cot)
    load("ids", ids_h, ids)
    load("gw", gw_h, gw)
    load("tok", tok_h, tok)
    load("hid", hid_h, hid)
    for p in range(4):
        load(f"w{p}", w_h.at[:, pl.ds(p * PAIR, PAIR)], w.at[:, pl.ds(p * PAIR, PAIR)])

    barrier = pltpu.get_barrier_semaphore()
    for dev in (n1p, n1m, n2p, n2m, zp, zm, pt):
        pl.semaphore_signal(barrier, inc=1, device_id=dev, device_id_type=MESH)

    copies = {}

    def send(key, src, dst, dev):
        k = len(copies)
        cp = pltpu.make_async_remote_copy(
            src_ref=src,
            dst_ref=dst,
            send_sem=send_sem.at[k],
            recv_sem=recv_sem.at[k],
            device_id=dev,
            device_id_type=MESH,
        )
        cp.start()
        copies[key] = cp

    def got(*key):
        copies[key].wait_recv()

    def crow(s, core, sub, n=SUB):
        return cotT.at[pl.ds(pl.multiple_of(zz(s) * ZBL + core * BLK + sub * SUB, 16), n)]

    loads["cot"].wait()
    own_row = pl.multiple_of(z * ZBL + c * BLK, 16)
    cotT[pl.ds(own_row, BLK), :] = dot(eye(BLK), cot[...], NT).astype(BF)
    pl.semaphore_wait(barrier, 7)
    send(("p", 0), crow(0, c, 0, BLK), crow(0, c, 0, BLK), pt)
    for sub in range(2):
        send(("u", 0, sub), crow(0, c, sub), crow(0, c, sub), zp)
        send(("d", 0, sub), crow(0, c, sub), crow(0, c, sub), zm)

    loads["ids"].wait()
    loads["gw"].wait()
    loads["tok"].wait()
    gate_col = jnp.sum(
        jnp.where(ids[...] == ei, gw[...].astype(F32), 0.0), axis=1, keepdims=True
    )
    it_t = lax.broadcasted_iota(jnp.int32, (TOK, ROWS), 0)
    it_r = lax.broadcasted_iota(jnp.int32, (TOK, ROWS), 1)
    live = (tok[...] == it_t) & (it_r < cnt_s[0, 0] * 128)
    gates = jnp.where(live, gate_col, 0.0).astype(BF)
    GT[...] = dot(eye(ROWS), gates, NT).astype(BF)

    loads["hid"].wait()
    for j in range(4):
        hT[256 * j : 256 * j + 256, :] = dot(
            eye(256), hid[:, 256 * j : 256 * j + 256], NT
        ).astype(BF)
    for r1 in range(4):
        for r2 in range(4):
            row = pl.multiple_of(64 * dpid((m1 + r1) % 4, (m2 + r2) % 4), 64)
            o = (r1 * 4 + r2) * 64
            hP[o : o + 64, :] = hT[pl.ds(row, 64), :]

    def ag(s, sub):
        got("u", s - 1, sub)
        src = crow(-s, c, sub)
        if s <= 2 or (s == 3 and sub == 0):
            send(("u", s, sub), src, src, zp)
        send(("pu", s, sub), src, src, pt)
        got("d", s - 1, sub)
        src = crow(s, c, sub)
        if s <= 2 or (s == 3 and sub == 1):
            send(("d", s, sub), src, src, zm)
        send(("pd", s, sub), src, src, pt)

    def ag_last():
        got("u", 3, 0)
        src = crow(-4, c, 0)
        send(("pu", 4, 0), src, src, pt)
        got("d", 3, 1)
        src = crow(4, c, 1)
        send(("pd", 4, 1), src, src, pt)

    def zrows(s):
        return cotT[pl.ds(pl.multiple_of(zz(s) * ZBL, 16), ZBL), :]

    def x1(k):
        if k == 0:
            got("p", 0)
        elif k == 4:
            got("pu", 4, 0)
            got("pd", 4, 1)
        else:
            for sub in range(2):
                got("pu", k, sub)
                got("pd", k, sub)
        wd = WIDTHS[k]
        if k in (0, 4):
            rows = jnp.concatenate([zrows(k), jnp.zeros((64, TOK), BF)], axis=0)
        else:
            rows = jnp.concatenate([zrows(k), zrows(-k)], axis=0)
        RT[:, 0:wd] = dot(GT[...], rows, NT).astype(BF)
        pb, rf, rn = PB[k], RF[k], RN[k]
        for r1 in (2, 1, 3, 0):
            pb[r1] = dot(hP[256 * r1 : 256 * r1 + 256, :], RT[:, 0:wd], NN).astype(BF)
            if r1 == 2:
                send(("F+", k), pb.at[2, pl.ds(0, 128)], rf.at[0], n1p)
                send(("F-", k), pb.at[2, pl.ds(128, 128)], rf.at[1], n1m)
            elif r1 == 1:
                send(("N+b", k), pb.at[1, pl.ds(128, 128)], rn.at[0, pl.ds(128, 128)], n1p)
            elif r1 == 3:
                send(("N-a", k), pb.at[3, pl.ds(0, 128)], rn.at[1, pl.ds(0, 128)], n1m)

    def x1b(k):
        pb, rf, rn = PB[k], RF[k], RN[k]
        got("F+", k)
        pb[1, 0:128, :] = (pb[1, 0:128, :].astype(F32) + rf[0].astype(F32)).astype(BF)
        send(("N+a", k), pb.at[1, pl.ds(0, 128)], rn.at[0, pl.ds(0, 128)], n1p)
        got("F-", k)
        pb[3, 128:256, :] = (pb[3, 128:256, :].astype(F32) + rf[1].astype(F32)).astype(BF)
        send(("N-b", k), pb.at[3, pl.ds(128, 128)], rn.at[1, pl.ds(128, 128)], n1m)

    def x2(k):
        pb, rn, s2, rf2, rn2 = PB[k], RN[k], S2[k], RF2[k], RN2[k]
        for key in ("N+b", "N-a", "N+a", "N-b"):
            got(key, k)
        for r2 in (2, 1, 3, 0):
            sl = slice(64 * r2, 64 * r2 + 64)
            tot = pb[0, sl, :].astype(F32) + rn[0, sl, :].astype(F32) + rn[1, sl, :].astype(F32)
            if r2 == 0:
                FB[k][...] = tot
            else:
                s2[r2] = tot.astype(BF)
            if r2 == 2:
                send(("f+", k), s2.at[2, pl.ds(0, 32)], rf2.at[0], n2p)
                send(("f-", k), s2.at[2, pl.ds(32, 32)], rf2.at[1], n2m)
            elif r2 == 1:
                send(("n+b", k), s2.at[1, pl.ds(32, 32)], rn2.at[0, pl.ds(32, 32)], n2p)
            elif r2 == 3:
                send(("n-a", k), s2.at[3, pl.ds(0, 32)], rn2.at[1, pl.ds(0, 32)], n2m)

    def x2b(k):
        s2, rf2, rn2 = S2[k], RF2[k], RN2[k]
        got("f+", k)
        s2[1, 0:32, :] = (s2[1, 0:32, :].astype(F32) + rf2[0].astype(F32)).astype(BF)
        send(("n+a", k), s2.at[1, pl.ds(0, 32)], rn2.at[0, pl.ds(0, 32)], n2p)
        got("f-", k)
        s2[3, 32:64, :] = (s2[3, 32:64, :].astype(F32) + rf2[1].astype(F32)).astype(BF)
        send(("n-b", k), s2.at[3, pl.ds(32, 32)], rn2.at[1, pl.ds(32, 32)], n2m)

    def x3(k):
        rn2 = RN2[k]
        for key in ("n+b", "n-a", "n+a", "n-b"):
            got(key, k)
        tot = FB[k][...] + rn2[0].astype(F32) + rn2[1].astype(F32)
        OZ[zz(k)] = tot[:, 0:512]
        if k in (1, 2, 3):
            OZ[zz(-k)] = pltpu.roll(tot[:, 384:896], 448, 1)

    def mixed(p):
        loads[f"w{p}"].wait()
        out = dot(hid[...], w[:, PAIR * p : PAIR * p + PAIR], NN).astype(BF)
        mt = dot(out, GT[...], TN).astype(BF)
        for k in range(2):
            for cc in range(2):
                o = ZBL * k + BLK * cc
                M[cc, 2 * p + k] = mt[o : o + BLK, :]
        send(("m", p), M.at[1 - c, pl.ds(2 * p, 2)], MR.at[pl.ds(2 * p, 2)], pt)

    def both(t, sl):
        return M[c, t, sl, :].astype(F32) + MR[t, sl, :].astype(F32)

    def rz(k):
        if k == 1:
            for p in range(4):
                got("m", p)
        for sub in range(2):
            sl = slice(SUB * sub, SUB * sub + SUB)
            for dirn, dev in ((0, zp), (1, zm)):
                if k == 1 and sub != dirn:
                    continue
                t = zz(5 - k) if dirn == 0 else zz(k - 5)
                v = both(t, sl)
                if k >= 3 or (k == 2 and sub == dirn):
                    got("z", dirn, k - 1, sub)
                    v = v + ZR[dirn, k - 2, sl, :].astype(F32)
                ZS[dirn, k - 1, sl, :] = v.astype(BF)
                send(
                    ("z", dirn, k, sub),
                    ZS.at[dirn, k - 1, pl.ds(SUB * sub, SUB)],
                    ZR.at[dirn, k - 1, pl.ds(SUB * sub, SUB)],
                    dev,
                )

    stores = []

    def store(src, dst):
        cp = pltpu.make_async_copy(src, dst, loc_sem.at[len(loads) + len(stores)])
        cp.start()
        stores.append(cp)

    def rz_last():
        for sub in range(2):
            for dirn in range(2):
                got("z", dirn, 4, sub)
        v = both(z, slice(0, BLK)) + ZR[0, 3].astype(F32) + ZR[1, 3].astype(F32)
        mixT[...] = v.astype(BF)
        mixb[...] = dot(eye(TOK), mixT[...], NT).astype(BF)
        store(mixb, mix_o)

    def hgrad(p):
        routed = dot(GT[...], cotT[PAIR * p : PAIR * p + PAIR, :], NT).astype(BF)
        part = dot(routed, w[:, PAIR * p : PAIR * p + PAIR], NT)
        if p == 0:
            acc[...] = part
        elif p < 3:
            acc[...] += part
        else:
            hgb[...] = (acc[...] + part).astype(BF)
            store(hgb, hg_o)

    x1(0)
    ag(1, 0)
    mixed(0)
    ag(1, 1)
    x1b(0)
    x1(1)
    ag(2, 0)
    mixed(1)
    x2(0)
    ag(2, 1)
    x1(2)
    x2b(0)
    ag(3, 0)
    mixed(2)
    ag(3, 1)
    x3(0)
    x1(3)
    x1b(1)
    mixed(3)
    ag_last()
    rz(1)
    x1(4)
    rz(2)
    x2(1)
    x1b(2)
    rz(3)
    hgrad(0)
    x2b(1)
    rz(4)
    x2(2)
    hgrad(1)
    x1b(3)
    x3(1)
    rz_last()
    x2b(2)
    hgrad(2)
    x2(3)
    x1b(4)
    x3(2)
    hgrad(3)
    x2b(3)
    x2(4)
    x3(3)
    x2b(4)
    x3(4)

    lane = lax.broadcasted_iota(jnp.int32, (64, 128), 1)
    for p in range(4):
        a, b = OZ[2 * p], pltpu.roll(OZ[2 * p + 1], 64, 1)
        o = PAIR * p
        wgb[:, o : o + 384] = a[:, 0:384]
        wgb[:, o + 384 : o + 512] = jnp.where(lane < 64, a[:, 384:512], b[:, 0:128])
        wgb[:, o + 512 : o + 896] = b[:, 128:512]
    store(wgb, wg_o)
    for cp in stores:
        cp.wait()
    for cp in copies.values():
        cp.wait_send()


def body(hidden, down_weight, cotangent, expert_ids, gate_weights, row_token, tile_count):
    v = pltpu.VMEM
    scratch = [
        v((ROWS, HID), BF),
        v((HID, ROWS), BF),
        v((HID, ROWS), BF),
        v((HID, DIM), BF),
        v((TOK, BLK), BF),
        v((TOK, 8), jnp.int32),
        v((TOK, 8), BF),
        v((1, ROWS), jnp.int32),
        v((ROWS, TOK), BF),
        v((DIM, TOK), BF),
        v((ROWS, PAIR), BF),
    ]
    scratch += [v((4, 256, n), BF) for n in WIDTHS]
    scratch += [v((2, 128, n), BF) for n in WIDTHS]
    scratch += [v((2, 256, n), BF) for n in WIDTHS]
    scratch += [v((4, 64, n), BF) for n in WIDTHS]
    scratch += [v((2, 32, n), BF) for n in WIDTHS]
    scratch += [v((2, 64, n), BF) for n in WIDTHS]
    scratch += [v((64, n), F32) for n in WIDTHS]
    scratch += [
        v((NZ, 64, 512), F32),
        v((64, DIM), F32),
        v((2, NZ, BLK, TOK), BF),
        v((NZ, BLK, TOK), BF),
        v((2, 4, BLK, TOK), BF),
        v((2, 4, BLK, TOK), BF),
        v((ROWS, HID), F32),
        v((ROWS, HID), BF),
        v((TOK, BLK), BF),
        v((BLK, TOK), BF),
        pltpu.SemaphoreType.DMA((N_COPIES,)),
        pltpu.SemaphoreType.DMA((N_COPIES,)),
        pltpu.SemaphoreType.DMA((16,)),
    ]
    hbm = pl.BlockSpec(memory_space=pl.ANY)
    mixed_out, hidden_grad, weight_grad = pl.pallas_call(
        kernel,
        out_shape=(
            jax.ShapeDtypeStruct((TOK, BLK), BF),
            jax.ShapeDtypeStruct((ROWS, HID), BF),
            jax.ShapeDtypeStruct((64, DIM), F32),
        ),
        in_specs=[hbm] * 6 + [pl.BlockSpec(memory_space=pltpu.SMEM)],
        out_specs=(hbm, hbm, hbm),
        scratch_shapes=scratch,
        compiler_params=pltpu.CompilerParams(
            collective_id=0, has_side_effects=True, vmem_limit_bytes=64_000_000
        ),
    )(
        hidden[0, 0],
        down_weight[0],
        cotangent,
        expert_ids,
        gate_weights,
        row_token[0],
        tile_count,
    )
    return mixed_out, hidden_grad[None, None], weight_grad[None]


def solution(mesh):
    placed = (
        P("dp", "expert", None, None),
        P("expert", None, None),
        P("dp", "expert"),
        P("dp", None),
        P("dp", None),
        P("dp", "expert", None),
        P("dp", "expert"),
    )
    return jax.shard_map(
        body,
        mesh=mesh,
        in_specs=placed,
        out_specs=(P("dp", "expert"), P("dp", "expert", None, None), P("expert", "dp", None)),
        check_vma=False,
    )
```

time: 316 us -> 86.8 us (0.27); the launches traced: 312 us -> 86.2 us
  waiting for transfers between devices: 137 us -> 0 us
  Pallas kernels: 0 us -> 74.1 us
  starting transfers between devices: 42 us -> 0 us
  matrix products: 38.6 us -> 0 us
  other arithmetic: 35.1 us -> 0 us
  local copies, waits for them, and re-layouts: 38.9 us -> 10.8 us
  between operations: 14.9 us -> 1.29 us
  loops' own time: 5.5 us -> 0 us
    ppermute x4 -> x0, waiting for transfers between devices: 96.2 us -> none  [swapped(): lax.ppermute(shard, axis, [(i, i ^ 1 << bit) for i in range(lax.axis_size...]
    pallas_call x0 -> x1, Pallas kernels: none -> 74.1 us  [body(): pl.pallas_call(kernel, out_shape=(jax.ShapeDtypeStruct((TOK, BLK), BF), j...]
    ppermute x4 -> x0, starting transfers between devices: 42 us -> none  [swapped(): lax.ppermute(shard, axis, [(i, i ^ 1 << bit) for i in range(lax.axis_size...]
    all_gather x1 -> x0, waiting for transfers between devices: 39.7 us -> none  [body(): group_cot = lax.all_gather(cotangent, 'expert', axis=1, tiled=True)]
    dot_general x7 -> x0, matrix products: 38.6 us -> none  [the longest x6 32.4 us: one_tile(): lax.dot_general(block, weight_mat, (((1,), (contract_dim,)), ((), ())), p...]
    gather x2 -> x0, local copies, waits for them, and re-layouts: 12.9 us -> none  [the longest x1 10.1 us: body(): group_cot[safe_rows].astype(jnp.float32)]
    scatter-add x1 -> x0, other arithmetic: 12.8 us -> none  [body(): partial_value.at[target]]
    convert_element_type x7 -> x0, other arithmetic: 11 us -> none  [the longest x4 6.2 us: body(): sending.astype(jnp.bfloat16)]
  transfers between devices with their start and end apart: 6 -> 0, of which waited for: 5 -> 0; matrix products, arithmetic and copies ran while one was open for 23% -> 0% of each run, Pallas kernels for 0% -> 0%
where the time goes in v1:
time: 86.8 us; the launch traced here: 86.2 us
  Pallas kernels  74.1 us (85%)
  local copies, waits for them, and re-layouts  10.8 us (12%)
  between operations  1.29 us (1%)
    pallas_call x1, Pallas kernels, body(): pl.pallas_call(kernel, out_shape=(jax.ShapeDtypeStruct((TOK, BLK), BF), j...  74.1 us
    unnamed x6, local copies, waits for them, and re-layouts  10.8 us

profile of v1, /device:TPU:8, one launch (start us, length us, event | category | flops | bytes accessed | tf_op | source)
XLA Modules:
  0.0 86.2 jit_solution(11100499870619095766)
XLA Ops:
  1.3 1.5 %copy.12.refs_4_ = bf16[512,8]{1,0:T(8,128)(2,1)} copy(bf16[512,8]{0,1:T(8,128)(2,1)} %param.11) | data formatting | bytes 16384 | tf_op args[4]
  2.8 1.8 %copy.10.refs_2_ = bf16[512,224]{1,0:T(8,128)(2,1)} copy(bf16[512,224]{0,1:T(8,128)(2,1)} %param.9) | data formatting | bytes 458752 | tf_op args[2]
  4.5 1.6 %copy.11.refs_3_ = s32[512,8]{1,0:T(8,128)} copy(s32[512,8]{0,1:T(8,128)} %param.10) | data formatting | bytes 32768 | tf_op args[3]
  6.1 74.1 %shard_map.94 = (bf16[512,224]{1,0:T(8,128)(2,1)}, bf16[384,1024]{1,0:T(8,128)(2,1)}, f32[64,3584]{1,0:T(8,128)}) custom-call(bf16[384,1024]{1,0:T(8,128)(2,1)} %bitcast.7, bf16[1024,3584]{1,0:T(8,128)(2,1)} %bitcast.5, bf16[512,224]{1,0:T(8,128)(2,1)} %copy.10.refs_2_, s32[512,8]{1,0:T(8,128)} %copy.11.refs_3_, bf16[512,8]{1,0:T(8,128)(2,1)} %copy.12.refs_4_, ...), custom_call_target="tpu_custom_call" | custom-call | tf_op jit(solution)/shard_map/pallas_call | solution.py:392
  80.2 1.8 %copy.13 = bf16[512,224]{0,1:T(8,128)(2,1)} copy(bf16[512,224]{1,0:T(8,128)(2,1)} %get-tuple-element.9) | data formatting | bytes 458752
  82.0 2.1 %copy.17 = bf16[1,1,384,1024]{3,2,1,0:T(8,128)(2,1)} copy(bf16[1,1,384,1024]{3,2,1,0:T(8,128)(2,1)} %bitcast.8) | data formatting | bytes 1572864
  84.0 2.2 %copy.18 = f32[1,64,3584]{2,1,0:T(8,128)} copy(f32[1,64,3584]{2,1,0:T(8,128)} %bitcast.6) | data formatting | bytes 1835008

commit v2 on v1

v2 whole, which is shorter than its diff:
```python
import jax
import jax.numpy as jnp
from jax import lax
from jax.experimental import pallas as pl
from jax.experimental.pallas import tpu as pltpu
from jax.sharding import PartitionSpec as P

MESH = pl.DeviceIdType.MESH
ROWS, HID, DIM, TOK = 384, 1024, 3584, 512
NZ = 8
BLK, SUB, ZBL, PAIR = 224, 112, 448, 896
CHUNKS = (
    ((0, 0, 384),),
    ((0, 384, 64), (1, 0, 112), (1, 224, 112), (-1, 0, 112), (-1, 224, 112)),
    ((1, 112, 112), (1, 336, 112), (-1, 112, 112), (-1, 336, 48)),
    ((-1, 384, 64), (2, 0, 448), (-2, 0, 384)),
    ((-2, 384, 64), (3, 0, 448), (-3, 0, 384)),
    ((-3, 384, 64), (4, 0, 448)),
)
WIDTHS = tuple(sum(n for _, _, n in pieces) for pieces in CHUNKS)
NCH = len(CHUNKS)
NT = (((1,), (1,)), ((), ()))
NN = (((1,), (0,)), ((), ()))
TN = (((0,), (0,)), ((), ()))
BF, F32 = jnp.bfloat16, jnp.float32
N_COPIES = 160


def dot(a, b, dims):
    return lax.dot_general(a, b, dims, preferred_element_type=F32)


def eye(n):
    return (
        lax.broadcasted_iota(jnp.int32, (n, n), 0) == lax.broadcasted_iota(jnp.int32, (n, n), 1)
    ).astype(F32).astype(BF)


def kernel(*refs):
    (hid_h, w_h, cot_h, ids_h, gw_h, tok_h, cnt_s, mix_o, hg_o, wg_o) = refs[:10]
    it = iter(refs[10:])
    nxt = lambda: next(it)
    hid, hT, hP, w, ids, gw, tok, GT, cotT = (nxt() for _ in range(9))
    RT = [nxt() for _ in range(NCH)]
    PB = [nxt() for _ in range(NCH)]
    RF = [nxt() for _ in range(NCH)]
    RN = [nxt() for _ in range(NCH)]
    S2 = [nxt() for _ in range(NCH)]
    RF2 = [nxt() for _ in range(NCH)]
    RN2 = [nxt() for _ in range(NCH)]
    FB = [nxt() for _ in range(NCH)]
    M, MR, ZS, ZR, acc = (nxt() for _ in range(5))
    mixT, hgb, OZ = mix_o, hg_o, wg_o
    send_sem, recv_sem, loc_sem = (nxt() for _ in range(3))

    dpi, ei = lax.axis_index("dp"), lax.axis_index("expert")
    x, y, z, c = dpi // 4, dpi % 4, ei // 2, ei % 2
    m1 = (1 - c) * x + c * y
    m2 = (1 - c) * y + c * x

    def dpid(p1, p2):
        return (1 - c) * (p1 * 4 + p2) + c * (p2 * 4 + p1)

    def zz(s):
        return (z + s + NZ) % NZ

    n1p = (dpid((m1 + 1) % 4, m2), ei)
    n1m = (dpid((m1 + 3) % 4, m2), ei)
    n2p = (dpid(m1, (m2 + 1) % 4), ei)
    n2m = (dpid(m1, (m2 + 3) % 4), ei)
    zp = (dpi, zz(1) * 2 + c)
    zm = (dpi, zz(-1) * 2 + c)
    pt = (dpi, z * 2 + 1 - c)

    loads = {}

    def load(name, src, dst):
        cp = pltpu.make_async_copy(src, dst, loc_sem.at[len(loads)])
        cp.start()
        loads[name] = cp

    own_row = pl.multiple_of(z * ZBL + c * BLK, 16)
    load("cot", cot_h, cotT.at[pl.ds(own_row, BLK)])
    load("ids", ids_h, ids)
    load("gw", gw_h, gw)
    load("tok", tok_h, tok)
    load("hid", hid_h, hid)
    for p in range(4):
        load(f"w{p}", w_h.at[:, pl.ds(p * PAIR, PAIR)], w.at[:, pl.ds(p * PAIR, PAIR)])

    barrier = pltpu.get_barrier_semaphore()
    for dev in (n1p, n1m, n2p, n2m, zp, zm, pt):
        pl.semaphore_signal(barrier, inc=1, device_id=dev, device_id_type=MESH)

    copies = {}

    def send(key, src, dst, dev):
        k = len(copies)
        cp = pltpu.make_async_remote_copy(
            src_ref=src,
            dst_ref=dst,
            send_sem=send_sem.at[k],
            recv_sem=recv_sem.at[k],
            device_id=dev,
            device_id_type=MESH,
        )
        cp.start()
        copies[key] = cp

    def got(*key):
        copies[key].wait_recv()

    def crow(s, core, sub, n=SUB):
        return cotT.at[pl.ds(pl.multiple_of(zz(s) * ZBL + core * BLK + sub * SUB, 16), n)]

    loads["cot"].wait()
    pl.semaphore_wait(barrier, 7)
    send(("p", 0), crow(0, c, 0, BLK), crow(0, c, 0, BLK), pt)
    for sub in range(2):
        send(("u", 0, sub), crow(0, c, sub), crow(0, c, sub), zp)
        send(("d", 0, sub), crow(0, c, sub), crow(0, c, sub), zm)

    loads["ids"].wait()
    loads["gw"].wait()
    loads["tok"].wait()
    gate_row = jnp.sum(
        jnp.where(ids[...] == ei, gw[...].astype(F32), 0.0), axis=0, keepdims=True
    )
    it_t = lax.broadcasted_iota(jnp.int32, (TOK, ROWS), 0)
    it_r = lax.broadcasted_iota(jnp.int32, (TOK, ROWS), 1)
    live = (tok[...] == it_t) & (it_r < cnt_s[0, 0] * 128)
    hot = jnp.where(live, 1.0, 0.0).astype(BF)
    GT[...] = (dot(eye(ROWS), hot, NT) * gate_row).astype(BF)

    loads["hid"].wait()
    for j in range(4):
        hT[256 * j : 256 * j + 256, :] = dot(
            eye(256), hid[:, 256 * j : 256 * j + 256], NT
        ).astype(BF)
    for r1 in range(4):
        for r2 in range(4):
            row = pl.multiple_of(64 * dpid((m1 + r1) % 4, (m2 + r2) % 4), 64)
            o = (r1 * 4 + r2) * 64
            hP[o : o + 64, :] = hT[pl.ds(row, 64), :]

    def ag(s, sub, dirn):
        got("ud"[dirn], s - 1, sub)
        src = crow(s if dirn else -s, c, sub)
        if s <= 2 or (s == 3 and sub == dirn):
            send(("ud"[dirn], s, sub), src, src, zm if dirn else zp)
        send(("p" + "ud"[dirn], s, sub), src, src, pt)

    def agl(dirn):
        got("ud"[dirn], 3, dirn)
        src = crow(4, c, dirn)
        send(("p" + "ud"[dirn], 4, dirn), src, src, pt)

    def x1a(k):
        if k == 0:
            got("p", 0)
        elif k == 5:
            got("pu", 4, 0)
            got("pd", 4, 1)
        else:
            for sub in {1: (0,), 2: (1,)}.get(k, (0, 1)):
                got("pu", max(k - 1, 1), sub)
                got("pd", max(k - 1, 1), sub)
        rows = [
            cotT[pl.ds(pl.multiple_of(zz(s) * ZBL + a, 16), n), :] for s, a, n in CHUNKS[k]
        ]
        rows = rows[0] if len(rows) == 1 else jnp.concatenate(rows, axis=0)
        RT[k][...] = dot(GT[...], rows, NT).astype(BF)
        pb, rf, rn = PB[k], RF[k], RN[k]
        for r1 in (2, 1, 3):
            pb[r1] = dot(hP[256 * r1 : 256 * r1 + 256, :], RT[k][...], NN).astype(BF)
            if r1 == 2:
                send(("F+", k), pb.at[2, pl.ds(0, 128)], rf.at[0], n1p)
                send(("F-", k), pb.at[2, pl.ds(128, 128)], rf.at[1], n1m)
            elif r1 == 1:
                send(("N+b", k), pb.at[1, pl.ds(128, 128)], rn.at[0, pl.ds(128, 128)], n1p)
            else:
                send(("N-a", k), pb.at[3, pl.ds(0, 128)], rn.at[1, pl.ds(0, 128)], n1m)

    def x1o(k):
        PB[k][0] = dot(hP[0:256, :], RT[k][...], NN).astype(BF)

    def x1b(k, dirn):
        pb, rf, rn = PB[k], RF[k], RN[k]
        if dirn == 0:
            got("F+", k)
            pb[1, 0:128, :] = (pb[1, 0:128, :].astype(F32) + rf[0].astype(F32)).astype(BF)
            send(("N+a", k), pb.at[1, pl.ds(0, 128)], rn.at[0, pl.ds(0, 128)], n1p)
        else:
            got("F-", k)
            pb[3, 128:256, :] = (pb[3, 128:256, :].astype(F32) + rf[1].astype(F32)).astype(BF)
            send(("N-b", k), pb.at[3, pl.ds(128, 128)], rn.at[1, pl.ds(128, 128)], n1m)

    def x2(k):
        pb, rn, s2, rf2, rn2 = PB[k], RN[k], S2[k], RF2[k], RN2[k]
        for key in ("N+b", "N-a", "N+a", "N-b"):
            got(key, k)
        for r2 in (2, 1, 3, 0):
            sl = slice(64 * r2, 64 * r2 + 64)
            tot = pb[0, sl, :].astype(F32) + rn[0, sl, :].astype(F32) + rn[1, sl, :].astype(F32)
            if r2 == 0:
                FB[k][...] = tot
            else:
                s2[r2] = tot.astype(BF)
            if r2 == 2:
                send(("f+", k), s2.at[2, pl.ds(0, 32)], rf2.at[0], n2p)
                send(("f-", k), s2.at[2, pl.ds(32, 32)], rf2.at[1], n2m)
            elif r2 == 1:
                send(("n+b", k), s2.at[1, pl.ds(32, 32)], rn2.at[0, pl.ds(32, 32)], n2p)
            elif r2 == 3:
                send(("n-a", k), s2.at[3, pl.ds(0, 32)], rn2.at[1, pl.ds(0, 32)], n2m)

    def x2b(k, dirn):
        s2, rf2, rn2 = S2[k], RF2[k], RN2[k]
        if dirn == 0:
            got("f+", k)
            s2[1, 0:32, :] = (s2[1, 0:32, :].astype(F32) + rf2[0].astype(F32)).astype(BF)
            send(("n+a", k), s2.at[1, pl.ds(0, 32)], rn2.at[0, pl.ds(0, 32)], n2p)
        else:
            got("f-", k)
            s2[3, 32:64, :] = (s2[3, 32:64, :].astype(F32) + rf2[1].astype(F32)).astype(BF)
            send(("n-b", k), s2.at[3, pl.ds(32, 32)], rn2.at[1, pl.ds(32, 32)], n2m)

    def x3(k):
        rn2 = RN2[k]
        for key in ("n+b", "n-a", "n+a", "n-b"):
            got(key, k)
        tot = FB[k][...] + rn2[0].astype(F32) + rn2[1].astype(F32)
        at = 0
        for s, a, n in CHUNKS[k]:
            OZ[zz(s), :, a : a + n] = tot[:, at : at + n]
            at += n

    def mixed(p):
        loads[f"w{p}"].wait()
        out = dot(hid[...], w[:, PAIR * p : PAIR * p + PAIR], NN).astype(BF)
        mt = dot(out, GT[...], TN).astype(BF)
        for k in range(2):
            for cc in range(2):
                o = ZBL * k + BLK * cc
                M[cc, 2 * p + k] = mt[o : o + BLK, :]
        send(("m", p), M.at[1 - c, pl.ds(2 * p, 2)], MR.at[pl.ds(2 * p, 2)], pt)

    def both(t, sl):
        return M[c, t, sl, :].astype(F32) + MR[t, sl, :].astype(F32)

    def rz(k, sub, dirn):
        if k == 1 and dirn == 0:
            for p in range(4):
                got("m", p)
        sl = slice(SUB * sub, SUB * sub + SUB)
        t = zz(k - 5) if dirn else zz(5 - k)
        v = both(t, sl)
        if k >= 3 or (k == 2 and sub == dirn):
            got("z", dirn, k - 1, sub)
            v = v + ZR[dirn, k - 2, sl, :].astype(F32)
        ZS[dirn, k - 1, sl, :] = v.astype(BF)
        send(
            ("z", dirn, k, sub),
            ZS.at[dirn, k - 1, pl.ds(SUB * sub, SUB)],
            ZR.at[dirn, k - 1, pl.ds(SUB * sub, SUB)],
            zm if dirn else zp,
        )

    def rzl():
        for sub in range(2):
            for dirn in range(2):
                got("z", dirn, 4, sub)
        v = both(z, slice(0, BLK)) + ZR[0, 3].astype(F32) + ZR[1, 3].astype(F32)
        mixT[...] = v.astype(BF)

    def hg(p):
        routed = dot(GT[...], cotT[PAIR * p : PAIR * p + PAIR, :], NT).astype(BF)
        part = dot(routed, w[:, PAIR * p : PAIR * p + PAIR], NT)
        if p == 0:
            acc[...] = part
        elif p < 3:
            acc[...] += part
        else:
            hgb[...] = (acc[...] + part).astype(BF)

    x1a(0)
    x1o(0)
    mixed(0)
    mixed(1)
    ag(1, 0, 0)
    ag(1, 0, 1)
    x1b(0, 0)
    x1b(0, 1)
    mixed(2)
    ag(1, 1, 0)
    ag(1, 1, 1)
    mixed(3)
    x2(0)
    x1a(1)
    x1a(2)
    ag(2, 0, 0)
    ag(2, 0, 1)
    rz(1, 0, 0)
    rz(1, 1, 1)
    rz(2, 0, 1)
    rz(2, 1, 0)
    x2b(0, 0)
    x2b(0, 1)
    x1o(1)
    x1o(2)
    ag(2, 1, 0)
    ag(2, 1, 1)
    x1b(1, 0)
    x1b(1, 1)
    x3(0)
    x1a(3)
    ag(3, 0, 0)
    ag(3, 0, 1)
    x1b(2, 0)
    x1b(2, 1)
    x1o(3)
    rz(2, 0, 0)
    rz(2, 1, 1)
    x2(1)
    rz(3, 1, 0)
    rz(3, 0, 1)
    x2b(1, 0)
    x2b(1, 1)
    x1b(3, 0)
    x1b(3, 1)
    ag(3, 1, 0)
    ag(3, 1, 1)
    x3(1)
    x1a(4)
    agl(0)
    x2(2)
    rz(3, 1, 1)
    x1o(4)
    rz(3, 0, 0)
    x2(3)
    rz(4, 0, 1)
    x2b(2, 0)
    x2b(2, 1)
    rz(4, 1, 0)
    agl(1)
    x2b(3, 0)
    x2b(3, 1)
    x1a(5)
    x1b(4, 0)
    x1b(4, 1)
    rz(4, 0, 0)
    rz(4, 1, 1)
    x1o(5)
    x3(2)
    hg(0)
    x3(3)
    hg(1)
    hg(2)
    x1b(5, 0)
    x1b(5, 1)
    hg(3)
    rzl()
    x2(4)
    x2(5)
    x2b(4, 0)
    x2b(4, 1)
    x2b(5, 0)
    x2b(5, 1)
    x3(4)
    x3(5)
    for cp in copies.values():
        cp.wait_send()


def finish(mix, hgr, blocks, mix_o, hg_o, wg_o, wgb, sem):
    first = pltpu.make_async_copy(hgr, hg_o, sem.at[4])
    second = pltpu.make_async_copy(mix, mix_o, sem.at[5])
    first.start()
    second.start()
    lane = lax.broadcasted_iota(jnp.int32, (64, 128), 1)
    rest = []
    for p in range(4):
        a, b = blocks[2 * p], pltpu.roll(blocks[2 * p + 1], 64, 1)
        o = PAIR * p
        wgb[:, o : o + 384] = a[:, 0:384]
        wgb[:, o + 384 : o + 512] = jnp.where(lane < 64, a[:, 384:512], b[:, 0:128])
        wgb[:, o + 512 : o + 896] = b[:, 128:512]
        cp = pltpu.make_async_copy(
            wgb.at[:, pl.ds(o, PAIR)], wg_o.at[:, pl.ds(o, PAIR)], sem.at[p]
        )
        cp.start()
        rest.append(cp)
    for cp in [first, second] + rest:
        cp.wait()


def body(hidden, down_weight, cotangent, expert_ids, gate_weights, row_token, tile_count):
    v = pltpu.VMEM
    scratch = [
        v((ROWS, HID), BF),
        v((HID, ROWS), BF),
        v((HID, ROWS), BF),
        v((HID, DIM), BF),
        v((8, TOK), jnp.int32),
        v((8, TOK), BF),
        v((1, ROWS), jnp.int32),
        v((ROWS, TOK), BF),
        v((DIM, TOK), BF),
    ]
    scratch += [v((ROWS, n), BF) for n in WIDTHS]
    scratch += [v((4, 256, n), BF) for n in WIDTHS]
    scratch += [v((2, 128, n), BF) for n in WIDTHS]
    scratch += [v((2, 256, n), BF) for n in WIDTHS]
    scratch += [v((4, 64, n), BF) for n in WIDTHS]
    scratch += [v((2, 32, n), BF) for n in WIDTHS]
    scratch += [v((2, 64, n), BF) for n in WIDTHS]
    scratch += [v((64, n), F32) for n in WIDTHS]
    scratch += [
        v((2, NZ, BLK, TOK), BF),
        v((NZ, BLK, TOK), BF),
        v((2, 4, BLK, TOK), BF),
        v((2, 4, BLK, TOK), BF),
        v((ROWS, HID), F32),
        pltpu.SemaphoreType.DMA((N_COPIES,)),
        pltpu.SemaphoreType.DMA((N_COPIES,)),
        pltpu.SemaphoreType.DMA((16,)),
    ]
    hbm = pl.BlockSpec(memory_space=pl.ANY)
    vm = pl.BlockSpec(memory_space=pltpu.VMEM)
    raw = pl.pallas_call(
        kernel,
        out_shape=(v((BLK, TOK), BF), v((ROWS, HID), BF), v((NZ, 64, 512), F32)),
        in_specs=[hbm] * 6 + [pl.BlockSpec(memory_space=pltpu.SMEM)],
        out_specs=(vm, vm, vm),
        scratch_shapes=scratch,
        compiler_params=pltpu.CompilerParams(
            collective_id=0, has_side_effects=True, vmem_limit_bytes=58_000_000
        ),
    )(
        hidden[0, 0],
        down_weight[0],
        cotangent.T,
        expert_ids.T,
        gate_weights.T,
        row_token[0],
        tile_count,
    )
    mixed_out, hidden_grad, weight_grad = pl.pallas_call(
        finish,
        out_shape=(
            jax.ShapeDtypeStruct((BLK, TOK), BF),
            jax.ShapeDtypeStruct((ROWS, HID), BF),
            jax.ShapeDtypeStruct((64, DIM), F32),
        ),
        in_specs=[vm] * 3,
        out_specs=(hbm,) * 3,
        scratch_shapes=[v((64, DIM), F32), pltpu.SemaphoreType.DMA((6,))],
        compiler_params=pltpu.CompilerParams(vmem_limit_bytes=4_000_000),
    )(*raw)
    return mixed_out.T, hidden_grad[None, None], weight_grad[None]


def solution(mesh):
    placed = (
        P("dp", "expert", None, None),
        P("expert", None, None),
        P("dp", "expert"),
        P("dp", None),
        P("dp", None),
        P("dp", "expert", None),
        P("dp", "expert"),
    )
    return jax.shard_map(
        body,
        mesh=mesh,
        in_specs=placed,
        out_specs=(P("dp", "expert"), P("dp", "expert", None, None), P("expert", "dp", None)),
        check_vma=False,
    )
```

time: 86.8 us -> 68.1 us (0.78)
  local copies, waits for them, and re-layouts: 10.8 us -> 0 us
  Pallas kernels: 74.1 us -> 66.5 us
    unnamed x6 -> x0, local copies, waits for them, and re-layouts: 10.8 us -> none
    pallas_call x1 -> x2, Pallas kernels: 74.1 us -> 66.5 us  [the longest x1 65.2 us: body(): pl.pallas_call(kernel, out_shape=(v((BLK, TOK), BF), v((ROWS, HID), BF),...]
where the time goes in v2:
time: 68.1 us; the launch traced here: 68 us
  Pallas kernels  66.5 us (98%)
  between operations  1.45 us (2%)
    pallas_call x1, Pallas kernels, body(): pl.pallas_call(kernel, out_shape=(v((BLK, TOK), BF), v((ROWS, HID), BF),...  65.2 us

profile of v2, /device:TPU:8, one launch (start us, length us, event | category | flops | bytes accessed | tf_op | source)
XLA Modules:
  0.0 68.0 jit_solution(438189625848437065)
XLA Ops:
  1.3 65.2 %shard_map.94 = (bf16[224,512]{1,0:T(8,128)(2,1)S(1)}, bf16[384,1024]{1,0:T(8,128)(2,1)S(1)}, f32[8,64,512]{2,1,0:T(8,128)S(1)}) custom-call(bf16[384,1024]{1,0:T(8,128)(2,1)} %bitcast.10, bf16[1024,3584]{1,0:T(8,128)(2,1)} %bitcast.9, bf16[224,512]{1,0:T(8,128)(2,1)} %bitcast.11, s32[8,512]{1,0:T(8,128)} %bitcast.12, bf16[8,512]{1,0:T(8,128)(2,1)} %bitcast.13, ...), custom_call_target="tpu_custom_call" | custom-call | tf_op jit(solution)/shard_map/pallas_call | solution.py:430
  66.5 1.3 %shard_map.95 = (bf16[224,512]{1,0:T(8,128)(2,1)}, bf16[384,1024]{1,0:T(8,128)(2,1)}, f32[64,3584]{1,0:T(8,128)}) custom-call(bf16[224,512]{1,0:T(8,128)(2,1)S(1)} %get-tuple-element.9.mix, bf16[384,1024]{1,0:T(8,128)(2,1)S(1)} %get-tuple-element.10.hgr, f32[8,64,512]{2,1,0:T(8,128)S(1)} %get-tuple-element.11.blocks), custom_call_target="tpu_custom_call" | custom-call | tf_op jit(solution)/shard_map/pallas_call | solution.py:448

commit v3 on v2

--- a/solution.py
+++ b/solution.py
@@ -11,19 +11,22 @@
 BLK, SUB, ZBL, PAIR = 224, 112, 448, 896
 CHUNKS = (
     ((0, 0, 384),),
-    ((0, 384, 64), (1, 0, 112), (1, 224, 112), (-1, 0, 112), (-1, 224, 112)),
-    ((1, 112, 112), (1, 336, 112), (-1, 112, 112), (-1, 336, 48)),
+    ((0, 384, 64), (1, 0, 80), (1, 224, 80), (-1, 0, 80), (-1, 224, 80)),
+    ((1, 80, 144), (1, 304, 144), (-1, 80, 144), (-1, 304, 80)),
     ((-1, 384, 64), (2, 0, 448), (-2, 0, 384)),
     ((-2, 384, 64), (3, 0, 448), (-3, 0, 384)),
-    ((-3, 384, 64), (4, 0, 448)),
+    ((-3, 384, 64), (4, 0, 320)),
+    ((4, 320, 128),),
 )
 WIDTHS = tuple(sum(n for _, _, n in pieces) for pieces in CHUNKS)
 NCH = len(CHUNKS)
+END = NCH - 1
+PIECE = (80, 144)
+N_SEND, N_RECV = 48, 74
 NT = (((1,), (1,)), ((), ()))
 NN = (((1,), (0,)), ((), ()))
 TN = (((0,), (0,)), ((), ()))
 BF, F32 = jnp.bfloat16, jnp.float32
-N_COPIES = 160
 
 
 def dot(a, b, dims):
@@ -68,6 +71,7 @@
     n1m = (dpid((m1 + 3) % 4, m2), ei)
     n2p = (dpid(m1, (m2 + 1) % 4), ei)
     n2m = (dpid(m1, (m2 + 3) % 4), ei)
+    n2f = (dpid(m1, (m2 + 2) % 4), ei)
     zp = (dpi, zz(1) * 2 + c)
     zm = (dpi, zz(-1) * 2 + c)
     pt = (dpi, z * 2 + 1 - c)
@@ -89,33 +93,58 @@
         load(f"w{p}", w_h.at[:, pl.ds(p * PAIR, PAIR)], w.at[:, pl.ds(p * PAIR, PAIR)])
 
     barrier = pltpu.get_barrier_semaphore()
-    for dev in (n1p, n1m, n2p, n2m, zp, zm, pt):
+    for dev in (n1p, n1m, n2p, n2m, n2f, zp, zm, pt):
         pl.semaphore_signal(barrier, inc=1, device_id=dev, device_id_type=MESH)
 
-    copies = {}
-
-    def send(key, src, dst, dev):
-        k = len(copies)
-        cp = pltpu.make_async_remote_copy(
+    slots, waited, sent = {}, set(), []
+
+    def group(key):
+        name, rest = key[0], key[1:]
+        if name in ("pu", "pd"):
+            return ("P",) + (rest if rest[0] == 1 else rest[:1])
+        if name == "m":
+            return ("m",)
+        if name == "z" and rest[1] == 4:
+            return ("Z", rest[0])
+        if name[0] in "Nn":
+            return (name[0], rest[0])
+        return key
+
+    def remote(src, dst, k, q, dev):
+        return pltpu.make_async_remote_copy(
             src_ref=src,
             dst_ref=dst,
             send_sem=send_sem.at[k],
-            recv_sem=recv_sem.at[k],
+            recv_sem=recv_sem.at[q],
             device_id=dev,
             device_id_type=MESH,
         )
+
+    def send(key, src, dst, dev):
+        q = slots.setdefault(group(key), len(slots))
+        k = len(sent)
+        if k >= N_SEND:
+            sent[k - N_SEND].wait_send()
+        cp = remote(src, dst, k % N_SEND, q, dev)
         cp.start()
-        copies[key] = cp
-
-    def got(*key):
-        copies[key].wait_recv()
-
-    def crow(s, core, sub, n=SUB):
-        return cotT.at[pl.ds(pl.multiple_of(zz(s) * ZBL + core * BLK + sub * SUB, 16), n)]
+        sent.append(cp)
+
+    def take(key, whole):
+        if key not in waited:
+            waited.add(key)
+            remote(whole, whole, 0, slots[key], pt).wait_recv()
+
+    def crow(s, core, sub):
+        at = pl.multiple_of(zz(s) * ZBL + core * BLK + sub * PIECE[0], 16)
+        return cotT.at[pl.ds(at, PIECE[sub])]
+
+    def span(n):
+        return cotT.at[pl.ds(0, n)]
 
     loads["cot"].wait()
-    pl.semaphore_wait(barrier, 7)
-    send(("p", 0), crow(0, c, 0, BLK), crow(0, c, 0, BLK), pt)
+    pl.semaphore_wait(barrier, 8)
+    own = cotT.at[pl.ds(own_row, BLK)]
+    send(("p", 0), own, own, pt)
     for sub in range(2):
         send(("u", 0, sub), crow(0, c, sub), crow(0, c, sub), zp)
         send(("d", 0, sub), crow(0, c, sub), crow(0, c, sub), zm)
@@ -144,27 +173,24 @@
             hP[o : o + 64, :] = hT[pl.ds(row, 64), :]
 
     def ag(s, sub, dirn):
-        got("ud"[dirn], s - 1, sub)
+        take(("ud"[dirn], s - 1, sub), span(PIECE[sub]))
         src = crow(s if dirn else -s, c, sub)
         if s <= 2 or (s == 3 and sub == dirn):
             send(("ud"[dirn], s, sub), src, src, zm if dirn else zp)
         send(("p" + "ud"[dirn], s, sub), src, src, pt)
 
     def agl(dirn):
-        got("ud"[dirn], 3, dirn)
+        take(("ud"[dirn], 3, dirn), span(PIECE[dirn]))
         src = crow(4, c, dirn)
         send(("p" + "ud"[dirn], 4, dirn), src, src, pt)
 
     def x1a(k):
         if k == 0:
-            got("p", 0)
-        elif k == 5:
-            got("pu", 4, 0)
-            got("pd", 4, 1)
-        else:
-            for sub in {1: (0,), 2: (1,)}.get(k, (0, 1)):
-                got("pu", max(k - 1, 1), sub)
-                got("pd", max(k - 1, 1), sub)
+            take(("p", 0), span(BLK))
+        elif k <= 2:
+            take(("P", 1, k - 1), span(2 * PIECE[k - 1]))
+        elif k < END:
+            take(("P", k - 1), span(BLK if k == 5 else 2 * BLK))
         rows = [
             cotT[pl.ds(pl.multiple_of(zz(s) * ZBL + a, 16), n), :] for s, a, n in CHUNKS[k]
         ]
@@ -187,18 +213,17 @@
     def x1b(k, dirn):
         pb, rf, rn = PB[k], RF[k], RN[k]
         if dirn == 0:
-            got("F+", k)
+            take(("F+", k), rf.at[0])
             pb[1, 0:128, :] = (pb[1, 0:128, :].astype(F32) + rf[0].astype(F32)).astype(BF)
             send(("N+a", k), pb.at[1, pl.ds(0, 128)], rn.at[0, pl.ds(0, 128)], n1p)
         else:
-            got("F-", k)
+            take(("F-", k), rf.at[1])
             pb[3, 128:256, :] = (pb[3, 128:256, :].astype(F32) + rf[1].astype(F32)).astype(BF)
             send(("N-b", k), pb.at[3, pl.ds(128, 128)], rn.at[1, pl.ds(128, 128)], n1m)
 
     def x2(k):
         pb, rn, s2, rf2, rn2 = PB[k], RN[k], S2[k], RF2[k], RN2[k]
-        for key in ("N+b", "N-a", "N+a", "N-b"):
-            got(key, k)
+        take(("N", k), rn)
         for r2 in (2, 1, 3, 0):
             sl = slice(64 * r2, 64 * r2 + 64)
             tot = pb[0, sl, :].astype(F32) + rn[0, sl, :].astype(F32) + rn[1, sl, :].astype(F32)
@@ -206,7 +231,12 @@
                 FB[k][...] = tot
             else:
                 s2[r2] = tot.astype(BF)
-            if r2 == 2:
+            if k == END:
+                if r2:
+                    to = (rn2.at[0], rf2, rn2.at[1])[r2 - 1]
+                    dev = (n2p, n2f, n2m)[r2 - 1]
+                    send((("n+", "ff", "n-")[r2 - 1], k), s2.at[r2], to, dev)
+            elif r2 == 2:
                 send(("f+", k), s2.at[2, pl.ds(0, 32)], rf2.at[0], n2p)
                 send(("f-", k), s2.at[2, pl.ds(32, 32)], rf2.at[1], n2m)
             elif r2 == 1:
@@ -217,19 +247,21 @@
     def x2b(k, dirn):
         s2, rf2, rn2 = S2[k], RF2[k], RN2[k]
         if dirn == 0:
-            got("f+", k)
+            take(("f+", k), rf2.at[0])
             s2[1, 0:32, :] = (s2[1, 0:32, :].astype(F32) + rf2[0].astype(F32)).astype(BF)
             send(("n+a", k), s2.at[1, pl.ds(0, 32)], rn2.at[0, pl.ds(0, 32)], n2p)
         else:
-            got("f-", k)
+            take(("f-", k), rf2.at[1])
             s2[3, 32:64, :] = (s2[3, 32:64, :].astype(F32) + rf2[1].astype(F32)).astype(BF)
             send(("n-b", k), s2.at[3, pl.ds(32, 32)], rn2.at[1, pl.ds(32, 32)], n2m)
 
     def x3(k):
         rn2 = RN2[k]
-        for key in ("n+b", "n-a", "n+a", "n-b"):
-            got(key, k)
+        take(("n", k), rn2)
         tot = FB[k][...] + rn2[0].astype(F32) + rn2[1].astype(F32)
+        if k == END:
+            take(("ff", k), RF2[k])
+            tot = tot + RF2[k][...].astype(F32)
         at = 0
         for s, a, n in CHUNKS[k]:
             OZ[zz(s), :, a : a + n] = tot[:, at : at + n]
@@ -249,14 +281,12 @@
         return M[c, t, sl, :].astype(F32) + MR[t, sl, :].astype(F32)
 
     def rz(k, sub, dirn):
-        if k == 1 and dirn == 0:
-            for p in range(4):
-                got("m", p)
+        take(("m",), MR)
         sl = slice(SUB * sub, SUB * sub + SUB)
         t = zz(k - 5) if dirn else zz(5 - k)
         v = both(t, sl)
         if k >= 3 or (k == 2 and sub == dirn):
-            got("z", dirn, k - 1, sub)
+            take(("z", dirn, k - 1, sub), ZR.at[dirn, k - 2, pl.ds(SUB * sub, SUB)])
             v = v + ZR[dirn, k - 2, sl, :].astype(F32)
         ZS[dirn, k - 1, sl, :] = v.astype(BF)
         send(
@@ -267,9 +297,8 @@
         )
 
     def rzl():
-        for sub in range(2):
-            for dirn in range(2):
-                got("z", dirn, 4, sub)
+        for dirn in range(2):
+            take(("Z", dirn), ZR.at[dirn, 3])
         v = both(z, slice(0, BLK)) + ZR[0, 3].astype(F32) + ZR[1, 3].astype(F32)
         mixT[...] = v.astype(BF)
 
@@ -285,90 +314,97 @@
 
     x1a(0)
     x1o(0)
-    mixed(0)
-    mixed(1)
     ag(1, 0, 0)
     ag(1, 0, 1)
     x1b(0, 0)
     x1b(0, 1)
+    x1a(1)
+    ag(1, 1, 1)
+    ag(1, 1, 0)
+    mixed(0)
+    x2(0)
+    ag(2, 0, 0)
+    x1a(2)
+    x1b(1, 1)
+    x1b(1, 0)
+    ag(2, 0, 1)
+    mixed(1)
+    x2b(0, 1)
+    x2b(0, 0)
+    x1o(2)
+    x1o(1)
+    ag(2, 1, 1)
+    ag(2, 1, 0)
+    x1b(2, 1)
+    x1b(2, 0)
+    x1a(3)
+    ag(3, 0, 0)
+    x3(0)
+    x2(1)
+    ag(3, 0, 1)
     mixed(2)
-    ag(1, 1, 0)
-    ag(1, 1, 1)
+    x2(2)
+    ag(3, 1, 1)
+    ag(3, 1, 0)
     mixed(3)
-    x2(0)
-    x1a(1)
-    x1a(2)
-    ag(2, 0, 0)
-    ag(2, 0, 1)
+    x2b(1, 0)
+    x2b(1, 1)
+    x2b(2, 1)
+    x1b(3, 1)
+    x2b(2, 0)
+    x1b(3, 0)
+    agl(0)
     rz(1, 0, 0)
     rz(1, 1, 1)
+    x1a(4)
+    agl(1)
     rz(2, 0, 1)
     rz(2, 1, 0)
-    x2b(0, 0)
-    x2b(0, 1)
-    x1o(1)
-    x1o(2)
-    ag(2, 1, 0)
-    ag(2, 1, 1)
-    x1b(1, 0)
-    x1b(1, 1)
-    x3(0)
-    x1a(3)
-    ag(3, 0, 0)
-    ag(3, 0, 1)
-    x1b(2, 0)
-    x1b(2, 1)
-    x1o(3)
+    x3(1)
+    x3(2)
+    x1a(5)
     rz(2, 0, 0)
+    x1a(6)
     rz(2, 1, 1)
-    x2(1)
+    hg(0)
     rz(3, 1, 0)
     rz(3, 0, 1)
-    x2b(1, 0)
-    x2b(1, 1)
-    x1b(3, 0)
-    x1b(3, 1)
-    ag(3, 1, 0)
-    ag(3, 1, 1)
-    x3(1)
-    x1a(4)
-    agl(0)
-    x2(2)
-    rz(3, 1, 1)
-    x1o(4)
-    rz(3, 0, 0)
-    x2(3)
-    rz(4, 0, 1)
-    x2b(2, 0)
-    x2b(2, 1)
-    rz(4, 1, 0)
-    agl(1)
-    x2b(3, 0)
-    x2b(3, 1)
-    x1a(5)
+    x1o(5)
     x1b(4, 0)
     x1b(4, 1)
+    hg(1)
+    rz(3, 0, 0)
+    hg(2)
+    x1o(6)
+    x1b(5, 0)
+    rz(3, 1, 1)
+    x1b(5, 1)
+    x1o(3)
+    x1o(4)
+    x1b(6, 1)
+    x1b(6, 0)
+    rz(4, 1, 0)
+    rz(4, 0, 1)
+    hg(3)
     rz(4, 0, 0)
+    x2(3)
+    x2(4)
     rz(4, 1, 1)
-    x1o(5)
-    x3(2)
-    hg(0)
-    x3(3)
-    hg(1)
-    hg(2)
-    x1b(5, 0)
-    x1b(5, 1)
-    hg(3)
-    rzl()
-    x2(4)
     x2(5)
+    x2b(3, 1)
+    x2(6)
+    x2b(3, 0)
     x2b(4, 0)
     x2b(4, 1)
     x2b(5, 0)
     x2b(5, 1)
+    x3(6)
+    x3(3)
     x3(4)
+    rzl()
     x3(5)
-    for cp in copies.values():
+    assert len(slots) == N_RECV
+    for cp in sent[-N_SEND:]:
         cp.wait_send()
 
 
@@ -412,7 +448,7 @@
     scratch += [v((2, 128, n), BF) for n in WIDTHS]
     scratch += [v((2, 256, n), BF) for n in WIDTHS]
     scratch += [v((4, 64, n), BF) for n in WIDTHS]
-    scratch += [v((2, 32, n), BF) for n in WIDTHS]
+    scratch += [v((2, 32, n), BF) for n in WIDTHS[:-1]] + [v((64, WIDTHS[-1]), BF)]
     scratch += [v((2, 64, n), BF) for n in WIDTHS]
     scratch += [v((64, n), F32) for n in WIDTHS]
     scratch += [
@@ -421,9 +457,9 @@
         v((2, 4, BLK, TOK), BF),
         v((2, 4, BLK, TOK), BF),
         v((ROWS, HID), F32),
-        pltpu.SemaphoreType.DMA((N_COPIES,)),
-        pltpu.SemaphoreType.DMA((N_COPIES,)),
-        pltpu.SemaphoreType.DMA((16,)),
+        pltpu.SemaphoreType.DMA((N_SEND,)),
+        pltpu.SemaphoreType.DMA((N_RECV,)),
+        pltpu.SemaphoreType.DMA((9,)),
     ]
     hbm = pl.BlockSpec(memory_space=pl.ANY)
     vm = pl.BlockSpec(memory_space=pltpu.VMEM)

time: 68.1 us -> 60.9 us (0.89); the launches traced: 68 us -> 60 us
  Pallas kernels: 66.5 us -> 58.6 us
    pallas_call x1, Pallas kernels: 65.2 us -> 57.3 us  [body(): pl.pallas_call(kernel, out_shape=(v((BLK, TOK), BF), v((ROWS, HID), BF),...]
where the time goes in v3:
time: 60.9 us; the launch traced here: 60 us
  Pallas kernels  58.6 us (96%)
  between operations  1.45 us (2%)
    pallas_call x1, Pallas kernels, body(): pl.pallas_call(kernel, out_shape=(v((BLK, TOK), BF), v((ROWS, HID), BF),...  57.3 us
    pallas_call x1, Pallas kernels, body(): pl.pallas_call(finish, out_shape=(jax.ShapeDtypeStruct((BLK, TOK), BF), j...  1.3 us

profile of v3, /device:TPU:8, one launch (start us, length us, event | category | flops | bytes accessed | tf_op | source)
XLA Modules:
  0.0 60.0 jit_solution(7405672763417854564)
XLA Ops:
  1.3 57.3 %shard_map.94 = (bf16[224,512]{1,0:T(8,128)(2,1)S(1)}, bf16[384,1024]{1,0:T(8,128)(2,1)S(1)}, f32[8,64,512]{2,1,0:T(8,128)S(1)}) custom-call(bf16[384,1024]{1,0:T(8,128)(2,1)} %bitcast.10, bf16[1024,3584]{1,0:T(8,128)(2,1)} %bitcast.9, bf16[224,512]{1,0:T(8,128)(2,1)} %bitcast.11, s32[8,512]{1,0:T(8,128)} %bitcast.12, bf16[8,512]{1,0:T(8,128)(2,1)} %bitcast.13, ...), custom_call_target="tpu_custom_call" | custom-call | tf_op jit(solution)/shard_map/pallas_call | solution.py:466
  58.5 1.3 %shard_map.95 = (bf16[224,512]{1,0:T(8,128)(2,1)}, bf16[384,1024]{1,0:T(8,128)(2,1)}, f32[64,3584]{1,0:T(8,128)}) custom-call(bf16[224,512]{1,0:T(8,128)(2,1)S(1)} %get-tuple-element.9.mix, bf16[384,1024]{1,0:T(8,128)(2,1)S(1)} %get-tuple-element.10.hgr, f32[8,64,512]{2,1,0:T(8,128)S(1)} %get-tuple-element.11.blocks), custom_call_target="tpu_custom_call" | custom-call | tf_op jit(solution)/shard_map/pallas_call | solution.py:484

commit v4 on v3

--- a/solution.py
+++ b/solution.py
@@ -22,7 +22,7 @@
 NCH = len(CHUNKS)
 END = NCH - 1
 PIECE = (80, 144)
-N_SEND, N_RECV = 48, 74
+N_SEND, N_RECV = 32, 74
 NT = (((1,), (1,)), ((), ()))
 NN = (((1,), (0,)), ((), ()))
 TN = (((0,), (0,)), ((), ()))
@@ -76,6 +76,10 @@
     zm = (dpi, zz(-1) * 2 + c)
     pt = (dpi, z * 2 + 1 - c)
 
+    barrier = pltpu.get_barrier_semaphore()
+    for dev in (n1p, n1m, n2p, n2m, n2f, zp, zm, pt):
+        pl.semaphore_signal(barrier, inc=1, device_id=dev, device_id_type=MESH)
+
     loads = {}
 
     def load(name, src, dst):
@@ -89,12 +93,6 @@
     load("gw", gw_h, gw)
     load("tok", tok_h, tok)
     load("hid", hid_h, hid)
-    for p in range(4):
-        load(f"w{p}", w_h.at[:, pl.ds(p * PAIR, PAIR)], w.at[:, pl.ds(p * PAIR, PAIR)])
-
-    barrier = pltpu.get_barrier_semaphore()
-    for dev in (n1p, n1m, n2p, n2m, n2f, zp, zm, pt):
-        pl.semaphore_signal(barrier, inc=1, device_id=dev, device_id_type=MESH)
 
     slots, waited, sent = {}, set(), []
 
@@ -141,14 +139,18 @@
     def span(n):
         return cotT.at[pl.ds(0, n)]
 
+    pl.semaphore_wait(barrier, 8)
+    for sub in range(2):
+        piece = cot_h.at[pl.ds(PIECE[0] * sub, PIECE[sub])]
+        send(("u", 0, sub), piece, crow(0, c, sub), zp)
+        send(("d", 0, sub), piece, crow(0, c, sub), zm)
+        if sub == 0:
+            send(("p", 0), cot_h, cotT.at[pl.ds(own_row, BLK)], pt)
+
+    for p in range(4):
+        load(f"w{p}", w_h.at[:, pl.ds(p * PAIR, PAIR)], w.at[:, pl.ds(p * PAIR, PAIR)])
+
     loads["cot"].wait()
-    pl.semaphore_wait(barrier, 8)
-    own = cotT.at[pl.ds(own_row, BLK)]
-    send(("p", 0), own, own, pt)
-    for sub in range(2):
-        send(("u", 0, sub), crow(0, c, sub), crow(0, c, sub), zp)
-        send(("d", 0, sub), crow(0, c, sub), crow(0, c, sub), zm)
-
     loads["ids"].wait()
     loads["gw"].wait()
     loads["tok"].wait()
@@ -312,98 +314,97 @@
         else:
             hgb[...] = (acc[...] + part).astype(BF)
 
+    mixed(0)
     x1a(0)
-    x1o(0)
     ag(1, 0, 0)
     ag(1, 0, 1)
+    mixed(1)
+    x1a(1)
+    x1b(0, 1)
+    ag(1, 1, 0)
     x1b(0, 0)
-    x1b(0, 1)
-    x1a(1)
     ag(1, 1, 1)
-    ag(1, 1, 0)
-    mixed(0)
+    mixed(2)
+    x1a(2)
+    x1o(0)
+    ag(2, 0, 1)
+    ag(2, 0, 0)
+    mixed(3)
     x2(0)
-    ag(2, 0, 0)
-    x1a(2)
+    x1b(1, 0)
+    x1o(1)
     x1b(1, 1)
-    x1b(1, 0)
-    ag(2, 0, 1)
-    mixed(1)
+    ag(2, 1, 0)
+    ag(2, 1, 1)
+    x1b(2, 1)
+    rz(1, 1, 1)
+    x1b(2, 0)
+    rz(1, 0, 0)
+    x1a(3)
+    ag(3, 0, 1)
+    ag(3, 0, 0)
+    x1o(2)
+    x2(1)
+    ag(3, 1, 0)
+    ag(3, 1, 1)
+    rz(2, 1, 0)
+    rz(2, 0, 1)
     x2b(0, 1)
+    x2(2)
     x2b(0, 0)
-    x1o(2)
-    x1o(1)
-    ag(2, 1, 1)
-    ag(2, 1, 0)
-    x1b(2, 1)
-    x1b(2, 0)
-    x1a(3)
-    ag(3, 0, 0)
-    x3(0)
-    x2(1)
-    ag(3, 0, 1)
-    mixed(2)
-    x2(2)
-    ag(3, 1, 1)
-    ag(3, 1, 0)
-    mixed(3)
     x2b(1, 0)
+    x1o(3)
+    x1a(4)
+    x1b(3, 1)
+    agl(1)
+    rz(2, 1, 1)
+    rz(2, 0, 0)
+    agl(0)
     x2b(1, 1)
-    x2b(2, 1)
-    x1b(3, 1)
-    x2b(2, 0)
+    rz(3, 1, 0)
     x1b(3, 0)
-    agl(0)
-    rz(1, 0, 0)
-    rz(1, 1, 1)
-    x1a(4)
-    agl(1)
-    rz(2, 0, 1)
-    rz(2, 1, 0)
-    x3(1)
-    x3(2)
+    rz(3, 0, 1)
     x1a(5)
-    rz(2, 0, 0)
     x1a(6)
-    rz(2, 1, 1)
     hg(0)
-    rz(3, 1, 0)
-    rz(3, 0, 1)
-    x1o(5)
     x1b(4, 0)
+    rz(3, 0, 0)
+    rz(3, 1, 1)
     x1b(4, 1)
     hg(1)
-    rz(3, 0, 0)
+    x3(0)
+    x1b(5, 1)
     hg(2)
-    x1o(6)
     x1b(5, 0)
-    rz(3, 1, 1)
-    x1b(5, 1)
-    x1o(3)
+    x1b(6, 0)
+    x3(1)
     x1o(4)
     x1b(6, 1)
-    x1b(6, 0)
     rz(4, 1, 0)
+    rz(4, 0, 0)
     rz(4, 0, 1)
-    hg(3)
-    rz(4, 0, 0)
+    x1o(5)
     x2(3)
+    x1o(6)
+    rz(4, 1, 1)
     x2(4)
-    rz(4, 1, 1)
     x2(5)
+    x2b(2, 0)
+    x2(6)
+    x2b(2, 1)
     x2b(3, 1)
-    x2(6)
     x2b(3, 0)
     x2b(4, 0)
     x2b(4, 1)
+    x2b(5, 1)
     x2b(5, 0)
-    x2b(5, 1)
+    hg(3)
+    rzl()
     x3(6)
     x3(3)
     x3(4)
-    rzl()
+    x3(2)
     x3(5)
-    assert len(slots) == N_RECV
     for cp in sent[-N_SEND:]:
         cp.wait_send()
 

time: 60.9 us -> 60.1 us (0.987)
  no operation moved by 1% of the time
where the time goes in v4:
time: 60.1 us; the launch traced here: 59.4 us
  Pallas kernels  58 us (97%)
  between operations  1.45 us (2%)
    pallas_call x1, Pallas kernels, body(): pl.pallas_call(kernel, out_shape=(v((BLK, TOK), BF), v((ROWS, HID), BF),...  56.7 us
    pallas_call x1, Pallas kernels, body(): pl.pallas_call(finish, out_shape=(jax.ShapeDtypeStruct((BLK, TOK), BF), j...  1.3 us

profile of v4, /device:TPU:8, one launch (start us, length us, event | category | flops | bytes accessed | tf_op | source)
XLA Modules:
  0.0 59.4 jit_solution(5333814760047208510)
XLA Ops:
  1.3 56.7 %shard_map.94 = (bf16[224,512]{1,0:T(8,128)(2,1)S(1)}, bf16[384,1024]{1,0:T(8,128)(2,1)S(1)}, f32[8,64,512]{2,1,0:T(8,128)S(1)}) custom-call(bf16[384,1024]{1,0:T(8,128)(2,1)} %bitcast.10, bf16[1024,3584]{1,0:T(8,128)(2,1)} %bitcast.9, bf16[224,512]{1,0:T(8,128)(2,1)} %bitcast.11, s32[8,512]{1,0:T(8,128)} %bitcast.12, bf16[8,512]{1,0:T(8,128)(2,1)} %bitcast.13, ...), custom_call_target="tpu_custom_call" | custom-call | tf_op jit(solution)/shard_map/pallas_call | solution.py:467
  57.9 1.3 %shard_map.95 = (bf16[224,512]{1,0:T(8,128)(2,1)}, bf16[384,1024]{1,0:T(8,128)(2,1)}, f32[64,3584]{1,0:T(8,128)}) custom-call(bf16[224,512]{1,0:T(8,128)(2,1)S(1)} %get-tuple-element.9.mix, bf16[384,1024]{1,0:T(8,128)(2,1)S(1)} %get-tuple-element.10.hgr, f32[8,64,512]{2,1,0:T(8,128)S(1)} %get-tuple-element.11.blocks), custom_call_target="tpu_custom_call" | custom-call | tf_op jit(solution)/shard_map/pallas_call | solution.py:485
